TPU v7x, 256 devices: a whole 4x4x8 slice. The times are simulated.
256 devices in a mesh: gx: 8 (over z), gy: 32 (over y, x, core).
Axes of the slice: x: 4, y: 4, z: 8, core: 2. Of those that a mesh axis runs over, the one named last changes fastest.
Arguments:
- child_coef: bfloat16 [512, 16, 128, 128], P(('gx', 'gy')), may hold values from -6 to 6
- transfer: bfloat16 [512, 64, 2, 128, 128], P(('gx', 'gy')), may hold values from -0.125 to 0.125
- child_dir: int32 [512, 64], P(('gx', 'gy')), may hold values from 0 to 15, as said below
- couple_src: int32 [64, 64, 7], P('gx', 'gy'), may hold values from 0 to 63, as said below
- couple_kind: int32 [64, 64, 7], P('gx', 'gy'), may hold values from 0 to 7
- couple_count: int32 [64, 64], P('gx', 'gy'), may hold values from 1 to 7, as said below
- couple_table: bfloat16 [64, 8, 2, 128, 128], P('gy'), may hold values from -0.1875 to 0.1875
Outputs:
- child_local: bfloat16 [512, 16, 128, 128], P(('gx', 'gy'))
Inputs may be any that keep to these rules, and one draw needn't show every extreme that they name: `child_dir`: in every row each child direction is named by exactly four parent directions. `couple_src`: the entries of one block row are distinct and never the row's own parent cluster. `couple_count`: some row holds 7.
All inputs are finite; a program needn't handle non-finite values.
Results may differ from a plain program's by a relative error of at most 0.015.
Values may be sent and summed in bfloat16 or wider, within the bound.
A program may use at most 128 MiB of HBM per device.

v0:
```python
import jax
import jax.numpy as jnp
from jax import lax
from jax.sharding import PartitionSpec as P

CPD = 2


def complex_apply(real_part, imag_part, vectors, pattern):
    halfway = vectors.shape[-1] // 2
    real_term = jnp.einsum(pattern, real_part, vectors, preferred_element_type=jnp.float32)
    imag_term = jnp.einsum(pattern, imag_part, vectors, preferred_element_type=jnp.float32)
    return jnp.concatenate(
        [
            real_term[..., :halfway] - imag_term[..., halfway:],
            real_term[..., halfway:] + imag_term[..., :halfway],
        ],
        axis=-1,
    )


def sum_groups(received):
    groups = received.shape[0] // (8 // CPD)
    merged = received.astype(jnp.float32).reshape((groups, 8 // CPD) + received.shape[1:])
    return jnp.sum(merged, axis=1).astype(jnp.bfloat16)


def body(child_coef, transfer, child_dir, couple_src, couple_kind, couple_count, couple_table):
    picked = jnp.take_along_axis(child_coef, child_dir[:, :, None, None], axis=1)
    upward = complex_apply(transfer[:, :, 0], transfer[:, :, 1], picked, "cers,cesa->cera")
    summed = jnp.sum(upward, axis=0, keepdims=True).astype(jnp.bfloat16)
    parent = sum_groups(lax.all_to_all(summed, "gy", split_axis=1, concat_axis=0, tiled=True))
    everything = lax.all_gather(parent, "gx", axis=0, tiled=True)
    dir_local = jnp.arange(parent.shape[1], dtype=jnp.int32)[None, :, None]
    sources = everything[couple_src, dir_local]
    matrices = couple_table[dir_local, couple_kind]
    products = complex_apply(
        matrices[:, :, :, 0], matrices[:, :, :, 1], sources, "uemrs,uemsa->uemra"
    )
    active = jnp.arange(couple_src.shape[-1], dtype=jnp.int32) < couple_count[..., None]
    parent_local = jnp.sum(jnp.where(active[..., None, None], products, 0.0), axis=2).astype(
        jnp.bfloat16
    )
    copies = jnp.repeat(parent_local, 8 // CPD, axis=0)
    parent_row = lax.all_to_all(copies, "gy", split_axis=0, concat_axis=1, tiled=True)[0]
    descent = complex_apply(transfer[:, :, 0], transfer[:, :, 1], parent_row, "cesr,esa->cera")
    child_index = jnp.arange(child_coef.shape[1], dtype=jnp.int32)
    onehot = (child_dir[:, None, :] == child_index[None, :, None]).astype(jnp.float32)
    child_local = jnp.einsum("cie,cera->cira", onehot, descent)
    return child_local.astype(jnp.bfloat16)


def solution(mesh):
    return jax.shard_map(
        body,
        mesh=mesh,
        in_specs=(
            P(("gx", "gy"), None, None, None),
            P(("gx", "gy"), None, None, None, None),
            P(("gx", "gy"), None),
            P("gx", "gy", None),
            P("gx", "gy", None),
            P("gx", "gy"),
            P("gy", None, None, None, None),
        ),
        out_specs=P(("gx", "gy"), None, None, None),
        check_vma=False,
    )
```

profile of v0, /device:TPU:1, one launch (start us, length us, event | category | flops | bytes accessed | tf_op | source)
XLA Modules:
  0.0 241.7 jit_solution(4865288829287410528)
XLA Ops:
  6.5 0.0 copy-start
  6.5 0.0 all-gather.2.cloned.1.call-start
  6.5 0.8 bitcast_or_fusion
  7.3 0.7 compare_and_fusion
  8.0 0.1 reshape.63
  8.1 4.3 %gather_fusion.2 = bf16[128,128,128]{2,1,0:T(8,128)(2,1)} fusion(bf16[2,16,128,128]{3,2,1,0:T(8,128)(2,1)} %param.7, s32[128]{0:T(128)S(1)} %reshape.63), kind=kCustom, calls=%fused_computation.2 | custom fusion | bytes 8389632 | tf_op jit(solution)/shard_map/jit(take_along_axis)/gather | solution.py:29
  12.4 6.3 %copy.35 = bf16[2,64,128,128]{2,3,1,0:T(8,128)(2,1)} copy(bf16[2,64,128,128]{3,2,1,0:T(8,128)(2,1)} %bitcast.69) | data formatting | bytes 8388608 | tf_op jit(solution)/shard_map/jit(take_along_axis)/gather | solution.py:29
  18.7 0.0 copy-start.2
  18.7 9.9 %fusion.10 = f32[2,64,128,128]{2,3,1,0:T(8,128)} fusion(bf16[2,64,128,128]{2,3,1,0:T(8,128)(2,1)} %copy.35, pred[2,64]{1,0:T(4,128)(4,1)S(1)} %compare_and_fusion, bf16[2,64,2,128,128]{4,3,2,1,0:T(8,128)(2,1)} %param.8), kind=kOutput, calls=%fused_computation.27 | convolution fusion | flops 538968064 | bytes 16777344 | tf_op jit(solution)/shard_map/cers,cesa->cera/dot_general | solution.py:12
  28.6 0.0 copy-done.2
  28.6 8.5 %fusion.9 = f32[2,64,128,128]{2,3,1,0:T(8,128)} fusion(bf16[2,64,128,128]{2,3,1,0:T(8,128)(2,1)S(1)} %copy-done.2, pred[2,64]{1,0:T(4,128)(4,1)S(1)} %compare_and_fusion, bf16[2,64,2,128,128]{4,3,2,1,0:T(8,128)(2,1)} %param.8), kind=kOutput, calls=%fused_computation.26 | convolution fusion | flops 538968064 | bytes 16777344 | tf_op jit(solution)/shard_map/cers,cesa->cera/dot_general | solution.py:11
  37.1 10.3 %slice_subtract_fusion.1 = (f32[2,64,128,64]{2,3,1,0:T(8,128)S(1)}, f32[2,64,128,64]{2,3,1,0:T(8,128)}) fusion(f32[2,64,128,128]{2,3,1,0:T(8,128)} %fusion.10, f32[2,64,128,128]{2,3,1,0:T(8,128)} %fusion.9), kind=kLoop, calls=%fused_computation.10 | loop fusion | flops 2097152 | bytes 25165824 | tf_op jit(solution)/shard_map/sub | solution.py:15
  47.5 5.0 %maximum_reduce_fusion = bf16[64,128,128]{1,2,0:T(8,128)(2,1)} fusion(f32[2,64,128,64]{2,3,1,0:T(8,128)} %get-tuple-element.8, f32[2,64,128,64]{2,3,1,0:T(8,128)S(1)} %get-tuple-element.7), kind=kLoop, calls=%fused_computation.3 | loop fusion | flops 3145728 | bytes 10485760 | tf_op jit(solution)/shard_map/reduce_sum | solution.py:31
  52.4 4.1 %copy.38 = bf16[1,64,128,128]{3,2,0,1:T(8,128)(2,1)} copy(bf16[1,64,128,128]{2,3,1,0:T(8,128)(2,1)} %bitcast.70) | data formatting | bytes 4194304 | tf_op jit(solution)/shard_map/convert_element_type | solution.py:31
  56.5 0.0 copy-start.7
  56.5 0.0 copy-start.8
  56.5 37.0 %all_to_all.21 = bf16[1,64,128,128]{3,2,0,1:T(8,128)(2,1)S(1)} all-to-all(bf16[1,64,128,128]{3,2,0,1:T(8,128)(2,1)} %copy.38), channel_id=1, replica_groups=mesh['gx'=8,'gy'=32] {'gy'}, dimensions={1} | all-to-all | bytes 4194304 | tf_op jit(solution)/shard_map/all_to_all | solution.py:32
  93.5 1.3 reduce_sum.31
  94.8 0.0 all-gather.2.cloned.1.call-update
  94.8 0.0 copy-done.7
  94.9 0.1 copy.39
  94.9 0.1 reshape.57
  95.0 0.0 copy-done.8
  95.1 0.1 copy.33
  95.2 0.1 reshape.51
  95.3 0.0 copy-done
  95.3 7.8 %gather_fusion = bf16[112,2,128,128]{3,2,1,0:T(8,128)(2,1)} fusion(bf16[2,8,2,128,128]{4,3,2,1,0:T(8,128)(2,1)S(1)} %copy-done, s32[112]{0:T(128)S(1)} %reshape.51), kind=kCustom, calls=%fused_computation | custom fusion | bytes 14680960 | tf_op jit(solution)/shard_map/gather | solution.py:36
  103.1 0.0 copy-start.9
  103.1 9.4 %copy.34 = bf16[112,2,128,128]{3,2,0,1:T(8,128)(2,1)} copy(bf16[112,2,128,128]{3,2,1,0:T(8,128)(2,1)} %gather_fusion) | data formatting | bytes 14680064 | tf_op jit(solution)/shard_map/gather | solution.py:36
  112.5 0.0 copy-done.9
  112.5 0.1 copy.32
  112.6 0.1 iota_compare_fusion.1
  112.6 36.0 %all-gather.2.cloned.1.call-done = bf16[64,2,128,128]{3,2,1,0:T(8,128)(2,1)} async-done(((bf16[8,2,128,128]{3,2,1,0:T(8,128)(2,1)}), bf16[64,2,128,128]{3,2,1,0:T(8,128)(2,1)}) %all-gather.2.cloned.1.call-update) | async-done | bytes 4194320 | tf_op jit(solution)/shard_map/all_gather | solution.py:33
  148.6 5.5 %gather_fusion.1 = bf16[112,128,128]{2,1,0:T(8,128)(2,1)} fusion(bf16[64,2,128,128]{3,2,1,0:T(8,128)(2,1)} %all-gather.2.cloned.1.call-done, s32[112]{0:T(128)S(1)} %reshape.57), kind=kCustom, calls=%fused_computation.1 | custom fusion | bytes 7340928 | tf_op jit(solution)/shard_map/gather | solution.py:35
  154.1 0.0 copy-start.3
  154.1 0.0 copy-start.4
  154.1 6.0 %fusion.7 = f32[8,2,7,128,128]{3,4,2,1,0:T(8,128)S(1)} fusion(bf16[8,2,7,128,128]{4,3,2,1,0:T(8,128)(2,1)} %bitcast.63, bf16[8,2,7,2,128,128]{5,4,2,1,0,3:T(8,128)(2,1)} %bitcast.65), kind=kOutput, calls=%fused_computation.23 | convolution fusion | flops 469762048 | bytes 14680064 | tf_op jit(solution)/shard_map/uemrs,uemsa->uemra/dot_general | solution.py:12
  160.1 0.0 copy-done.3
  160.1 0.3 copy-done.4
  160.5 5.6 %fusion.8 = f32[8,2,7,128,128]{3,4,2,1,0:T(8,128)} fusion(bf16[8,2,7,128,128]{4,3,2,1,0:T(8,128)(2,1)S(1)} %bitcast.64, bf16[8,2,7,2,128,128]{5,4,2,1,0,3:T(8,128)(2,1)S(1)} %bitcast.66), kind=kOutput, calls=%fused_computation.25 | convolution fusion | flops 469762048 | bytes 14680064 | tf_op jit(solution)/shard_map/uemrs,uemsa->uemra/dot_general | solution.py:11
  166.1 7.7 %slice_subtract_fusion.2 = (f32[8,2,7,128,64]{3,4,2,1,0:T(8,128)S(1)}, f32[8,2,7,128,64]{3,4,2,1,0:T(8,128)}) fusion(f32[8,2,7,128,128]{3,4,2,1,0:T(8,128)S(1)} %fusion.7, f32[8,2,7,128,128]{3,4,2,1,0:T(8,128)} %fusion.8), kind=kLoop, calls=%fused_computation.21 | loop fusion | flops 1835008 | bytes 22020096 | tf_op jit(solution)/shard_map/sub | solution.py:15
  173.8 2.8 %fusion = bf16[8,2,128,128]{2,3,1,0:T(8,128)(2,1)S(1)} fusion(f32[8,2,7,128,64]{3,4,2,1,0:T(8,128)} %get-tuple-element.10, f32[8,2,7,128,64]{3,4,2,1,0:T(8,128)S(1)} %get-tuple-element.9, pred[8,2,7]{2,1,0:T(4,128)(4,1)S(1)} %iota_compare_fusion.1), kind=kLoop, calls=%fused_computation.6 | loop fusion | flops 5242880 | bytes 7864432 | tf_op jit(solution)/shard_map/reduce_sum | solution.py:41
  176.6 1.9 broadcast_in_dim.55
  178.5 7.7 %all-to-all-start.1 = ((bf16[32,2,128,128]{2,3,1,0:T(8,128)(2,1)}), bf16[32,2,128,128]{2,3,1,0:T(8,128)(2,1)S(1)}, u32[]{:S(2)}, u32[]{:S(2)}) async-start(bf16[32,2,128,128]{2,3,1,0:T(8,128)(2,1)} %bitcast.71), calls=%async_computation.1 | async-start | bytes 4194304 | tf_op jit(solution)/shard_map/all_to_all | solution.py:45
  186.2 6.1 %slice_bitcast_fusion.1 = (bf16[2,64,128,128]{3,2,1,0:T(8,128)(2,1)}, bf16[2,64,128,128]{3,2,1,0:T(8,128)(2,1)}) fusion(bf16[2,64,2,128,128]{4,3,2,1,0:T(8,128)(2,1)} %param.8), kind=kLoop, calls=%fused_computation.16 | loop fusion | bytes 16777216 | tf_op jit(solution)/shard_map/squeeze | solution.py:30
  192.3 22.5 %all-to-all-done.1 = bf16[32,2,128,128]{2,3,1,0:T(8,128)(2,1)S(1)} async-done(((bf16[32,2,128,128]{2,3,1,0:T(8,128)(2,1)}), bf16[32,2,128,128]{2,3,1,0:T(8,128)(2,1)S(1)}, u32[]{:S(2)}, u32[]{:S(2)}) %all-to-all-start.1) | async-done | bytes 2097184 | tf_op jit(solution)/shard_map/all_to_all | solution.py:45
  214.8 0.0 copy-start.5
  214.8 3.6 %fusion.11 = f32[2,64,128,128]{2,3,0,1:T(8,128)S(1)} fusion(bf16[64,128,128,1]{1,2,3,0:T(8,128)(2,1)S(1)} %bitcast.67, bf16[2,64,128,128]{3,2,1,0:T(8,128)(2,1)} %get-tuple-element.11), kind=kOutput, calls=%fused_computation.28 | convolution fusion | flops 536870912 | bytes 14680064 | tf_op jit(solution)/shard_map/cesr,esa->cera/dot_general | solution.py:11
  218.4 0.0 copy-done.5
  218.4 1.2 fusion.14
  219.7 2.1 slice_subtract_fusion
  221.8 2.3 pad_maximum_fusion
  224.0 0.0 copy-start.6
  224.0 0.0 copy-start.1
  224.0 6.7 %copy.44 = bf16[2,64,128,128]{3,1,2,0:T(8,128)(2,1)} copy(bf16[2,64,128,128]{2,3,0,1:T(8,128)(2,1)} %pad_maximum_fusion) | data formatting | bytes 8388608 | tf_op jit(solution)/shard_map/concatenate | solution.py:13
  230.7 0.0 copy-done.6
  230.7 2.8 %convolution_convert_fusion = bf16[2,16,128,128]{3,1,2,0:T(8,128)(2,1)S(1)} fusion(bf16[2,64,128,128]{3,1,2,0:T(8,128)(2,1)} %copy.44, s32[2,64]{1,0:T(2,128)S(1)} %copy-done.6), kind=kOutput, calls=%fused_computation.33 | convolution fusion | flops 67110912 | bytes 5243392 | tf_op jit(solution)/shard_map/cie,cera->cira/dot_general | solution.py:49
  233.6 1.2 copy.45
  234.8 0.0 copy-done.1
  (2 shorter events, 0.0 us)
Async XLA Ops:
  6.5 88.7 %copy-start = (bf16[2,8,2,128,128]{4,3,2,1,0:T(8,128)(2,1)S(1)}, bf16[2,8,2,128,128]{4,3,2,1,0:T(8,128)(2,1)}, u32[]{:S(2)}) copy-start(bf16[2,8,2,128,128]{4,3,2,1,0:T(8,128)(2,1)} %param.13) | copy-start | bytes 3145732
  6.5 142.1 %all-gather.2.cloned.1.call-start = ((), (), s32[]{:S(2)}) async-start(), calls=%async_computation.2 | async-start | bytes 4718592 | tf_op jit(solution)/shard_map/all_gather | solution.py:33
  18.7 9.9 %copy-start.2 = (bf16[2,64,128,128]{2,3,1,0:T(8,128)(2,1)S(1)}, bf16[2,64,128,128]{2,3,1,0:T(8,128)(2,1)}, u32[]{:S(2)}) copy-start(bf16[2,64,128,128]{2,3,1,0:T(8,128)(2,1)} %copy.35) | copy-start | bytes 12582916
  56.5 38.3 %copy-start.7 = (s32[8,2,7]{0,1,2:T(2,128)S(1)}, s32[8,2,7]{0,1,2:T(2,128)}, u32[]{:S(2)}) copy-start(s32[8,2,7]{0,1,2:T(2,128)} %param.10) | copy-start | bytes 1348
  56.5 38.6 %copy-start.8 = (s32[8,2,7]{0,1,2:T(2,128)S(1)}, s32[8,2,7]{0,1,2:T(2,128)}, u32[]{:S(2)}) copy-start(s32[8,2,7]{0,1,2:T(2,128)} %param.11) | copy-start | bytes 1348
  103.1 9.4 %copy-start.9 = (s32[8,2]{0,1:T(2,128)S(1)}, s32[8,2]{0,1:T(2,128)}, u32[]{:S(2)}) copy-start(s32[8,2]{0,1:T(2,128)} %param.12) | copy-start | bytes 196
  154.1 6.0 %copy-start.3 = (bf16[112,128,128]{2,1,0:T(8,128)(2,1)S(1)}, bf16[112,128,128]{2,1,0:T(8,128)(2,1)}, u32[]{:S(2)}) copy-start(bf16[112,128,128]{2,1,0:T(8,128)(2,1)} %gather_fusion.1) | copy-start | bytes 11010052
  154.1 6.3 %copy-start.4 = (bf16[112,2,128,128]{3,2,0,1:T(8,128)(2,1)S(1)}, bf16[112,2,128,128]{3,2,0,1:T(8,128)(2,1)}, u32[]{:S(2)}) copy-start(bf16[112,2,128,128]{3,2,0,1:T(8,128)(2,1)} %copy.34) | copy-start | bytes 22020100
  178.5 36.3 %all-to-all-start.1 = ((bf16[32,2,128,128]{2,3,1,0:T(8,128)(2,1)}), bf16[32,2,128,128]{2,3,1,0:T(8,128)(2,1)S(1)}, u32[]{:S(2)}, u32[]{:S(2)}) async-start(bf16[32,2,128,128]{2,3,1,0:T(8,128)(2,1)} %bitcast.71), calls=%async_computation.1 | async-start | bytes 4194304 | tf_op jit(solution)/shard_map/all_to_all | solution.py:45
  214.8 3.6 %copy-start.5 = (bf16[2,64,128,128]{3,2,1,0:T(8,128)(2,1)S(1)}, bf16[2,64,128,128]{3,2,1,0:T(8,128)(2,1)}, u32[]{:S(2)}) copy-start(bf16[2,64,128,128]{3,2,1,0:T(8,128)(2,1)} %get-tuple-element.12) | copy-start | bytes 12582916
  224.0 6.7 %copy-start.6 = (s32[2,64]{1,0:T(2,128)S(1)}, s32[2,64]{1,0:T(2,128)}, u32[]{:S(2)}) copy-start(s32[2,64]{1,0:T(2,128)} %param.9) | copy-start | bytes 1540
  224.0 10.8 %copy-start.1 = (bf16[2,8,2,128,128]{4,3,2,1,0:T(8,128)(2,1)S(1)}, bf16[2,8,2,128,128]{4,3,2,1,0:T(8,128)(2,1)}, u32[]{:S(2)}) copy-start(bf16[2,8,2,128,128]{4,3,2,1,0:T(8,128)(2,1)} %param.13) | copy-start | bytes 3145732
Sparse Core Ops, SparseCore 0:
  94.9 53.6 all-gather.1
where the time goes:
time: 242 us
  waiting for transfers between devices  58.5 us (24%)
  local copies, waits for them, and re-layouts  54.2 us (22%)
  matrix products  37.7 us (16%)
  blocking collectives  37 us (15%)
  other arithmetic  33 us (14%)
  between operations  13.5 us (6%)
  starting transfers between devices  7.7 us (3%)
    all_to_all x1, blocking collectives, body(): lax.all_to_all(summed, 'gy', split_axis=1, concat_axis=0, tiled=True)  37 us
    all_gather x1, waiting for transfers between devices, body(): everything = lax.all_gather(parent, 'gx', axis=0, tiled=True)  36 us
    all_to_all x1, waiting for transfers between devices, body(): lax.all_to_all(copies, 'gy', split_axis=0, concat_axis=1, tiled=True)[0]  22.5 us
    sub x3, other arithmetic, complex_apply(): real_term[..., :halfway] - imag_term[..., halfway:]  20.1 us
    dot_general x3, matrix products, complex_apply(): jnp.einsum(pattern, real_part, vectors, preferred_element_type=jnp.float32)  17.7 us
    gather x2, local copies, waits for them, and re-layouts, body(): matrices = couple_table[dir_local, couple_kind]  17.2 us
    dot_general x3, matrix products, complex_apply(): jnp.einsum(pattern, imag_part, vectors, preferred_element_type=jnp.float32)  17.2 us
    gather x3, local copies, waits for them, and re-layouts, body(): jnp.take_along_axis(child_coef, child_dir[:, :, None, None], axis=1)  10.7 us
  transfers between devices with their start and end apart: 2, of which 2 were waited for; matrix products, arithmetic and copies ran while one was open for 10% of the time, Pallas kernels for 0%

commit v1 on v0

--- a/solution.py
+++ b/solution.py
@@ -30,7 +30,9 @@
     upward = complex_apply(transfer[:, :, 0], transfer[:, :, 1], picked, "cers,cesa->cera")
     summed = jnp.sum(upward, axis=0, keepdims=True).astype(jnp.bfloat16)
     parent = sum_groups(lax.all_to_all(summed, "gy", split_axis=1, concat_axis=0, tiled=True))
-    everything = lax.all_gather(parent, "gx", axis=0, tiled=True)
+    everything = jnp.concatenate(
+        lax.all_to_all(jnp.stack([parent] * lax.axis_size("gx")), "gx", 0, 0), axis=0
+    )
     dir_local = jnp.arange(parent.shape[1], dtype=jnp.int32)[None, :, None]
     sources = everything[couple_src, dir_local]
     matrices = couple_table[dir_local, couple_kind]

time: 242 us -> 281 us (1.16)
  waiting for transfers between devices: 58.5 us -> 102 us
  between operations: 13.5 us -> 0.11 us
  starting transfers between devices: 7.7 us -> 12.8 us
  local copies, waits for them, and re-layouts: 54.2 us -> 58.2 us
    all_to_all x0 -> x1, waiting for transfers between devices: none -> 79.2 us  [body(): lax.all_to_all(jnp.stack([parent] * lax.axis_size('gx')), 'gx', 0, 0)]
    all_gather x1 -> x0, waiting for transfers between devices: 36 us -> none  [body(): everything = lax.all_gather(parent, 'gx', axis=0, tiled=True)]
    all_to_all x0 -> x1, starting transfers between devices: none -> 8.33 us  [body(): lax.all_to_all(jnp.stack([parent] * lax.axis_size('gx')), 'gx', 0, 0)]
    another operation x0 -> x1, local copies, waits for them, and re-layouts: none -> 4.13 us  [body(): jnp.stack([parent] * lax.axis_size('gx'))]
    all_to_all x1, starting transfers between devices: 7.7 us -> 4.45 us  [body(): lax.all_to_all(copies, 'gy', split_axis=0, concat_axis=1, tiled=True)[0]]
  transfers between devices with their start and end apart: 2 -> 2, of which waited for: 2 -> 2; matrix products, arithmetic and copies ran while one was open for 10% -> 8% of each run, Pallas kernels for 0% -> 0%
where the time goes in v1:
time: 281 us; the launch traced here: 280 us
  waiting for transfers between devices  102 us (36%)
  local copies, waits for them, and re-layouts  58.2 us (21%)
  matrix products  37.7 us (13%)
  blocking collectives  36.8 us (13%)
  other arithmetic  32.8 us (12%)
  starting transfers between devices  12.8 us (5%)
    all_to_all x1, waiting for transfers between devices, body(): lax.all_to_all(jnp.stack([parent] * lax.axis_size('gx')), 'gx', 0, 0)  79.2 us
    all_to_all x1, blocking collectives, body(): lax.all_to_all(summed, 'gy', split_axis=1, concat_axis=0, tiled=True)  36.8 us
    all_to_all x1, waiting for transfers between devices, body(): lax.all_to_all(copies, 'gy', split_axis=0, concat_axis=1, tiled=True)[0]  22.6 us
    sub x3, other arithmetic, complex_apply(): real_term[..., :halfway] - imag_term[..., halfway:]  20.1 us
    dot_general x3, matrix products, complex_apply(): jnp.einsum(pattern, real_part, vectors, preferred_element_type=jnp.float32)  17.7 us
    dot_general x3, matrix products, complex_apply(): jnp.einsum(pattern, imag_part, vectors, preferred_element_type=jnp.float32)  17.2 us
    gather x2, local copies, waits for them, and re-layouts, body(): matrices = couple_table[dir_local, couple_kind]  17 us
    gather x3, local copies, waits for them, and re-layouts, body(): jnp.take_along_axis(child_coef, child_dir[:, :, None, None], axis=1)  10.7 us
  transfers between devices with their start and end apart: 2, of which 2 were waited for; matrix products, arithmetic and copies ran while one was open for 8% of the time, Pallas kernels for 0%

profile of v1, /device:TPU:1, one launch (start us, length us, event | category | flops | bytes accessed | tf_op | source)
XLA Modules:
  0.0 280.2 jit_solution(12785140527498448354)
XLA Ops:
  0.0 0.0 copy-start
  0.0 0.8 bitcast_or_fusion
  0.8 0.7 compare_and_fusion
  1.5 0.1 reshape.69
  1.5 4.3 %gather_fusion.2 = bf16[128,128,128]{2,1,0:T(8,128)(2,1)} fusion(bf16[2,16,128,128]{3,2,1,0:T(8,128)(2,1)} %param.7, s32[128]{0:T(128)S(1)} %reshape.69), kind=kCustom, calls=%fused_computation.2 | custom fusion | bytes 8389632 | tf_op jit(solution)/shard_map/jit(take_along_axis)/gather | solution.py:29
  5.8 6.3 %copy.35 = bf16[2,64,128,128]{2,3,1,0:T(8,128)(2,1)} copy(bf16[2,64,128,128]{3,2,1,0:T(8,128)(2,1)} %bitcast.70) | data formatting | bytes 8388608 | tf_op jit(solution)/shard_map/jit(take_along_axis)/gather | solution.py:29
  12.2 0.0 copy-start.2
  12.2 9.9 %fusion.10 = f32[2,64,128,128]{2,3,1,0:T(8,128)} fusion(bf16[2,64,128,128]{2,3,1,0:T(8,128)(2,1)} %copy.35, pred[2,64]{1,0:T(4,128)(4,1)S(1)} %compare_and_fusion, bf16[2,64,2,128,128]{4,3,2,1,0:T(8,128)(2,1)} %param.8), kind=kOutput, calls=%fused_computation.27 | convolution fusion | flops 538968064 | bytes 16777344 | tf_op jit(solution)/shard_map/cers,cesa->cera/dot_general | solution.py:12
  22.1 0.0 copy-done.2
  22.1 8.5 %fusion.9 = f32[2,64,128,128]{2,3,1,0:T(8,128)} fusion(bf16[2,64,128,128]{2,3,1,0:T(8,128)(2,1)S(1)} %copy-done.2, pred[2,64]{1,0:T(4,128)(4,1)S(1)} %compare_and_fusion, bf16[2,64,2,128,128]{4,3,2,1,0:T(8,128)(2,1)} %param.8), kind=kOutput, calls=%fused_computation.26 | convolution fusion | flops 538968064 | bytes 16777344 | tf_op jit(solution)/shard_map/cers,cesa->cera/dot_general | solution.py:11
  30.6 10.3 %slice_subtract_fusion.1 = (f32[2,64,128,64]{2,3,1,0:T(8,128)S(1)}, f32[2,64,128,64]{2,3,1,0:T(8,128)}) fusion(f32[2,64,128,128]{2,3,1,0:T(8,128)} %fusion.10, f32[2,64,128,128]{2,3,1,0:T(8,128)} %fusion.9), kind=kLoop, calls=%fused_computation.10 | loop fusion | flops 2097152 | bytes 25165824 | tf_op jit(solution)/shard_map/sub | solution.py:15
  40.9 5.0 %maximum_reduce_fusion = bf16[64,128,128]{1,2,0:T(8,128)(2,1)} fusion(f32[2,64,128,64]{2,3,1,0:T(8,128)} %get-tuple-element.8, f32[2,64,128,64]{2,3,1,0:T(8,128)S(1)} %get-tuple-element.7), kind=kLoop, calls=%fused_computation.3 | loop fusion | flops 3145728 | bytes 10485760 | tf_op jit(solution)/shard_map/reduce_sum | solution.py:31
  45.9 4.1 %copy.38 = bf16[1,64,128,128]{3,2,0,1:T(8,128)(2,1)} copy(bf16[1,64,128,128]{2,3,1,0:T(8,128)(2,1)} %bitcast.71) | data formatting | bytes 4194304 | tf_op jit(solution)/shard_map/convert_element_type | solution.py:31
  49.9 36.8 %all_to_all.26 = bf16[1,64,128,128]{3,2,0,1:T(8,128)(2,1)S(1)} all-to-all(bf16[1,64,128,128]{3,2,0,1:T(8,128)(2,1)} %copy.38), channel_id=1, replica_groups=mesh['gx'=8,'gy'=32] {'gy'}, dimensions={1} | all-to-all | bytes 4194304 | tf_op jit(solution)/shard_map/all_to_all | solution.py:32
  86.8 1.3 reduce_sum.31
  88.1 4.1 %stack.2 = bf16[8,8,2,128,128]{4,3,2,1,0:T(8,128)(2,1)} broadcast(bf16[8,2,128,128]{3,2,1,0:T(8,128)(2,1)} %reduce_sum.31), dimensions={1,2,3,4} | broadcast | bytes 4718592 | tf_op jit(solution)/shard_map/stack | solution.py:34
  92.2 0.0 copy-start.7
  92.2 0.0 copy-start.8
  92.2 8.3 %all-to-all-start.1 = ((bf16[8,8,2,128,128]{4,3,2,1,0:T(8,128)(2,1)}), bf16[8,8,2,128,128]{4,3,2,1,0:T(8,128)(2,1)}, u32[]{:S(2)}, u32[]{:S(2)}) async-start(bf16[8,8,2,128,128]{4,3,2,1,0:T(8,128)(2,1)} %stack.2), calls=%async_computation.1 | async-start | bytes 8388608 | tf_op jit(solution)/shard_map/all_to_all | solution.py:34
  100.6 0.0 copy-done.7
  100.6 0.1 copy.39
  100.7 0.1 reshape.63
  100.8 0.0 copy-done.8
  100.8 0.1 copy.33
  100.9 0.1 reshape.57
  101.0 0.0 copy-done
  101.0 7.8 %gather_fusion = bf16[112,2,128,128]{3,2,1,0:T(8,128)(2,1)} fusion(bf16[2,8,2,128,128]{4,3,2,1,0:T(8,128)(2,1)S(1)} %copy-done, s32[112]{0:T(128)S(1)} %reshape.57), kind=kCustom, calls=%fused_computation | custom fusion | bytes 14680960 | tf_op jit(solution)/shard_map/gather | solution.py:38
  108.8 0.0 copy-start.9
  108.8 9.2 %copy.34 = bf16[112,2,128,128]{3,2,0,1:T(8,128)(2,1)} copy(bf16[112,2,128,128]{3,2,1,0:T(8,128)(2,1)} %gather_fusion) | data formatting | bytes 14680064 | tf_op jit(solution)/shard_map/gather | solution.py:38
  118.1 0.0 copy-done.9
  118.1 0.1 copy.32
  118.1 0.1 iota_compare_fusion.1
  118.2 79.2 %all-to-all-done.1 = bf16[8,8,2,128,128]{4,3,2,1,0:T(8,128)(2,1)} async-done(((bf16[8,8,2,128,128]{4,3,2,1,0:T(8,128)(2,1)}), bf16[8,8,2,128,128]{4,3,2,1,0:T(8,128)(2,1)}, u32[]{:S(2)}, u32[]{:S(2)}) %all-to-all-start.1) | async-done | bytes 4194336 | tf_op jit(solution)/shard_map/all_to_all | solution.py:34
  197.5 5.5 %gather_fusion.1 = bf16[112,128,128]{2,1,0:T(8,128)(2,1)} fusion(bf16[64,2,128,128]{3,2,1,0:T(8,128)(2,1)} %bitcast.13, s32[112]{0:T(128)S(1)} %reshape.63), kind=kCustom, calls=%fused_computation.1 | custom fusion | bytes 7340928 | tf_op jit(solution)/shard_map/gather | solution.py:37
  203.0 0.0 copy-start.3
  203.0 0.0 copy-start.4
  203.0 6.0 %fusion.7 = f32[8,2,7,128,128]{3,4,2,1,0:T(8,128)S(1)} fusion(bf16[8,2,7,128,128]{4,3,2,1,0:T(8,128)(2,1)} %bitcast.64, bf16[8,2,7,2,128,128]{5,4,2,1,0,3:T(8,128)(2,1)} %bitcast.66), kind=kOutput, calls=%fused_computation.23 | convolution fusion | flops 469762048 | bytes 14680064 | tf_op jit(solution)/shard_map/uemrs,uemsa->uemra/dot_general | solution.py:12
  209.0 0.0 copy-done.3
  209.0 0.3 copy-done.4
  209.3 5.6 %fusion.8 = f32[8,2,7,128,128]{3,4,2,1,0:T(8,128)} fusion(bf16[8,2,7,128,128]{4,3,2,1,0:T(8,128)(2,1)S(1)} %bitcast.65, bf16[8,2,7,2,128,128]{5,4,2,1,0,3:T(8,128)(2,1)S(1)} %bitcast.67), kind=kOutput, calls=%fused_computation.25 | convolution fusion | flops 469762048 | bytes 14680064 | tf_op jit(solution)/shard_map/uemrs,uemsa->uemra/dot_general | solution.py:11
  215.0 7.7 %slice_subtract_fusion.2 = (f32[8,2,7,128,64]{3,4,2,1,0:T(8,128)S(1)}, f32[8,2,7,128,64]{3,4,2,1,0:T(8,128)}) fusion(f32[8,2,7,128,128]{3,4,2,1,0:T(8,128)S(1)} %fusion.7, f32[8,2,7,128,128]{3,4,2,1,0:T(8,128)} %fusion.8), kind=kLoop, calls=%fused_computation.21 | loop fusion | flops 1835008 | bytes 22020096 | tf_op jit(solution)/shard_map/sub | solution.py:15
  222.7 2.6 fusion
  225.3 1.9 broadcast_in_dim.55
  227.2 4.5 %all-to-all-start.2 = ((bf16[32,2,128,128]{2,3,1,0:T(8,128)(2,1)}), bf16[32,2,128,128]{2,3,1,0:T(8,128)(2,1)S(1)}, u32[]{:S(2)}, u32[]{:S(2)}) async-start(bf16[32,2,128,128]{2,3,1,0:T(8,128)(2,1)} %bitcast.72), calls=%async_computation.2 | async-start | bytes 4194304 | tf_op jit(solution)/shard_map/all_to_all | solution.py:47
  231.6 6.1 %slice_bitcast_fusion.1 = (bf16[2,64,128,128]{3,2,1,0:T(8,128)(2,1)}, bf16[2,64,128,128]{3,2,1,0:T(8,128)(2,1)}) fusion(bf16[2,64,2,128,128]{4,3,2,1,0:T(8,128)(2,1)} %param.8), kind=kLoop, calls=%fused_computation.16 | loop fusion | bytes 16777216 | tf_op jit(solution)/shard_map/squeeze | solution.py:30
  237.7 22.6 %all-to-all-done.2 = bf16[32,2,128,128]{2,3,1,0:T(8,128)(2,1)S(1)} async-done(((bf16[32,2,128,128]{2,3,1,0:T(8,128)(2,1)}), bf16[32,2,128,128]{2,3,1,0:T(8,128)(2,1)S(1)}, u32[]{:S(2)}, u32[]{:S(2)}) %all-to-all-start.2) | async-done | bytes 2097184 | tf_op jit(solution)/shard_map/all_to_all | solution.py:47
  260.2 0.0 copy-start.5
  260.2 3.6 %fusion.11 = f32[2,64,128,128]{2,3,0,1:T(8,128)S(1)} fusion(bf16[64,128,128,1]{1,2,3,0:T(8,128)(2,1)S(1)} %bitcast.68, bf16[2,64,128,128]{3,2,1,0:T(8,128)(2,1)} %get-tuple-element.11), kind=kOutput, calls=%fused_computation.28 | convolution fusion | flops 536870912 | bytes 14680064 | tf_op jit(solution)/shard_map/cesr,esa->cera/dot_general | solution.py:11
  263.8 0.0 copy-done.5
  263.8 1.2 fusion.14
  265.1 2.1 slice_subtract_fusion
  267.2 2.3 pad_maximum_fusion
  269.5 0.0 copy-start.6
  269.5 0.0 copy-start.1
  269.5 6.7 %copy.44 = bf16[2,64,128,128]{3,1,2,0:T(8,128)(2,1)} copy(bf16[2,64,128,128]{2,3,0,1:T(8,128)(2,1)} %pad_maximum_fusion) | data formatting | bytes 8388608 | tf_op jit(solution)/shard_map/concatenate | solution.py:13
  276.1 0.0 copy-done.6
  276.1 2.8 %convolution_convert_fusion = bf16[2,16,128,128]{3,1,2,0:T(8,128)(2,1)S(1)} fusion(bf16[2,64,128,128]{3,1,2,0:T(8,128)(2,1)} %copy.44, s32[2,64]{1,0:T(2,128)S(1)} %copy-done.6), kind=kOutput, calls=%fused_computation.33 | convolution fusion | flops 67110912 | bytes 5243392 | tf_op jit(solution)/shard_map/cie,cera->cira/dot_general | solution.py:51
  279.0 1.2 copy.45
  280.2 0.0 copy-done.1
  (2 shorter events, 0.0 us)
Async XLA Ops:
  0.0 101.0 %copy-start = (bf16[2,8,2,128,128]{4,3,2,1,0:T(8,128)(2,1)S(1)}, bf16[2,8,2,128,128]{4,3,2,1,0:T(8,128)(2,1)}, u32[]{:S(2)}) copy-start(bf16[2,8,2,128,128]{4,3,2,1,0:T(8,128)(2,1)} %param.13) | copy-start | bytes 3145732
  12.2 9.9 %copy-start.2 = (bf16[2,64,128,128]{2,3,1,0:T(8,128)(2,1)S(1)}, bf16[2,64,128,128]{2,3,1,0:T(8,128)(2,1)}, u32[]{:S(2)}) copy-start(bf16[2,64,128,128]{2,3,1,0:T(8,128)(2,1)} %copy.35) | copy-start | bytes 12582916
  92.2 8.3 %copy-start.7 = (s32[8,2,7]{0,1,2:T(2,128)S(1)}, s32[8,2,7]{0,1,2:T(2,128)}, u32[]{:S(2)}) copy-start(s32[8,2,7]{0,1,2:T(2,128)} %param.10) | copy-start | bytes 1348
  92.2 8.6 %copy-start.8 = (s32[8,2,7]{0,1,2:T(2,128)S(1)}, s32[8,2,7]{0,1,2:T(2,128)}, u32[]{:S(2)}) copy-start(s32[8,2,7]{0,1,2:T(2,128)} %param.11) | copy-start | bytes 1348
  92.2 105.2 %all-to-all-start.1 = ((bf16[8,8,2,128,128]{4,3,2,1,0:T(8,128)(2,1)}), bf16[8,8,2,128,128]{4,3,2,1,0:T(8,128)(2,1)}, u32[]{:S(2)}, u32[]{:S(2)}) async-start(bf16[8,8,2,128,128]{4,3,2,1,0:T(8,128)(2,1)} %stack.2), calls=%async_computation.1 | async-start | bytes 8388608 | tf_op jit(solution)/shard_map/all_to_all | solution.py:34
  108.8 9.2 %copy-start.9 = (s32[8,2]{0,1:T(2,128)S(1)}, s32[8,2]{0,1:T(2,128)}, u32[]{:S(2)}) copy-start(s32[8,2]{0,1:T(2,128)} %param.12) | copy-start | bytes 196
  203.0 6.0 %copy-start.3 = (bf16[112,128,128]{2,1,0:T(8,128)(2,1)S(1)}, bf16[112,128,128]{2,1,0:T(8,128)(2,1)}, u32[]{:S(2)}) copy-start(bf16[112,128,128]{2,1,0:T(8,128)(2,1)} %gather_fusion.1) | copy-start | bytes 11010052
  203.0 6.3 %copy-start.4 = (bf16[112,2,128,128]{3,2,0,1:T(8,128)(2,1)S(1)}, bf16[112,2,128,128]{3,2,0,1:T(8,128)(2,1)}, u32[]{:S(2)}) copy-start(bf16[112,2,128,128]{3,2,0,1:T(8,128)(2,1)} %copy.34) | copy-start | bytes 22020100
  227.2 33.1 %all-to-all-start.2 = ((bf16[32,2,128,128]{2,3,1,0:T(8,128)(2,1)}), bf16[32,2,128,128]{2,3,1,0:T(8,128)(2,1)S(1)}, u32[]{:S(2)}, u32[]{:S(2)}) async-start(bf16[32,2,128,128]{2,3,1,0:T(8,128)(2,1)} %bitcast.72), calls=%async_computation.2 | async-start | bytes 4194304 | tf_op jit(solution)/shard_map/all_to_all | solution.py:47
  260.2 3.6 %copy-start.5 = (bf16[2,64,128,128]{3,2,1,0:T(8,128)(2,1)S(1)}, bf16[2,64,128,128]{3,2,1,0:T(8,128)(2,1)}, u32[]{:S(2)}) copy-start(bf16[2,64,128,128]{3,2,1,0:T(8,128)(2,1)} %get-tuple-element.12) | copy-start | bytes 12582916
  269.5 6.7 %copy-start.6 = (s32[2,64]{1,0:T(2,128)S(1)}, s32[2,64]{1,0:T(2,128)}, u32[]{:S(2)}) copy-start(s32[2,64]{1,0:T(2,128)} %param.9) | copy-start | bytes 1540
  269.5 10.8 %copy-start.1 = (bf16[2,8,2,128,128]{4,3,2,1,0:T(8,128)(2,1)S(1)}, bf16[2,8,2,128,128]{4,3,2,1,0:T(8,128)(2,1)}, u32[]{:S(2)}) copy-start(bf16[2,8,2,128,128]{4,3,2,1,0:T(8,128)(2,1)} %param.13) | copy-start | bytes 3145732
